TPU v7x, 32 devices: a whole 2x2x4 slice. The times are simulated.
32 devices in a mesh: wide: 8 (over y, x, core), narrow: 4 (over z).
Axes of the slice: x: 2, y: 2, z: 4, core: 2. Of those that a mesh axis runs over, the one named last changes fastest.
Arguments:
- events: bfloat16 [8192, 1024], P('wide'), may hold values from -36 to 36
- lengths: int32 [24], replicated, may hold values from 1 to 2048, 8192 in all
- in_gain: float32 [1024], replicated, may hold values from 0.1 to 1.9
- w_uvqk: bfloat16 [1024, 8, 512], P(None, 'narrow'), may hold values from -2 to 2, as said below
- out_gain: float32 [8, 128], P('narrow'), may hold values from 0.1 to 1.9
- w_out: bfloat16 [8, 128, 1024], P('narrow'), may hold values from -0.25 to 0.25
Outputs:
- layer_out: bfloat16 [8192, 1024], P('wide', 'narrow')
Inputs may be any that keep to these rules, and one draw needn't show every extreme that they name: `w_uvqk`: projection weights.
All inputs are finite; a program needn't handle non-finite values.
Results may differ from a plain program's by a relative error of at most 0.0036.
Values may be sent and summed in bfloat16 or wider, within the bound.
A program may use at most 64 MiB of HBM per device.

v0:
```python
import jax
import jax.numpy as jnp
from jax import lax
from jax.sharding import PartitionSpec as P


def from_behind(value, axis, steps):
    count = lax.axis_size(axis)
    initial, last = (max(0, -steps), min(count, count - steps))
    return lax.ppermute(value, axis, [(source, source + steps) for source in range(initial, last)])


def fetch_relay(pair):
    return from_behind((pair[0], pair[1]), "wide", 1)


def on_device(events, lengths, in_gain, w_uvqk, out_gain, w_out):
    rows_w = events.shape[0]
    heads_local = w_uvqk.shape[1]
    head_size = out_gain.shape[1]
    events_f = events.astype(jnp.float32)
    average = jnp.mean(events_f, axis=-1, keepdims=True)
    variance = jnp.mean((events_f - average) ** 2, axis=-1, keepdims=True)
    normed = ((events_f - average) * lax.rsqrt(variance + 1e-05) * in_gain).astype(jnp.bfloat16)
    projected = jnp.einsum("rd,dhc->rhc", normed, w_uvqk, preferred_element_type=jnp.float32)
    projected = jax.nn.silu(projected).astype(jnp.bfloat16)
    update_gate = projected[:, :, :head_size]
    values_own = projected[:, :, head_size : 2 * head_size]
    queries = projected[:, :, 2 * head_size : 3 * head_size]
    keys_own = projected[:, :, 3 * head_size :]
    user_ends = jnp.cumsum(lengths)

    def owner_of(grow):
        return jnp.sum((user_ends[None, :] <= grow[:, None]).astype(jnp.int32), axis=1)

    first_row = lax.axis_index("wide") * rows_w
    query_pos = first_row + jnp.arange(rows_w, dtype=jnp.int32)
    query_user = owner_of(query_pos)
    scaling = head_size ** (-0.5)

    def attend(running, key_rows, value_rows, key_first):
        key_count = key_rows.shape[0]
        block_rows = 512

        def block_step(carry, block_index):
            key_start = block_index * block_rows
            key_block = lax.dynamic_slice_in_dim(key_rows, key_start, block_rows, 0)
            value_block = lax.dynamic_slice_in_dim(value_rows, key_start, block_rows, 0)
            key_pos = key_first + key_start + jnp.arange(block_rows, dtype=jnp.int32)
            key_user = owner_of(key_pos)
            allowed = (
                (key_user[None, :] == query_user[:, None])
                & (key_pos[None, :] <= query_pos[:, None])
                & (key_pos[None, :] >= 0)
            )
            scores = (
                jnp.einsum("rhc,khc->hrk", queries, key_block, preferred_element_type=jnp.float32)
                * scaling
            )
            weights = jnp.where(allowed[None], jax.nn.silu(scores), 0.0).astype(jnp.bfloat16)
            carry = carry + jnp.einsum(
                "hrk,khc->rhc", weights, value_block, preferred_element_type=jnp.float32
            )
            return (carry, None)

        running, _ = lax.scan(
            block_step, running, jnp.arange(key_count // block_rows, dtype=jnp.int32)
        )
        return running

    attended = attend(
        jnp.zeros((rows_w, heads_local, head_size), jnp.float32), keys_own, values_own, first_row
    )
    reach = lax.axis_size("wide") // 4

    def relay_turn(turn_index, carry):
        keys_held, values_held, running = carry
        keys_held, values_held = fetch_relay((keys_held, values_held))
        running = attend(running, keys_held, values_held, first_row - turn_index * rows_w)
        return (keys_held, values_held, running)

    _, _, attended = lax.fori_loop(1, reach + 1, relay_turn, (keys_own, values_own, attended))
    centre = jnp.mean(attended, axis=-1, keepdims=True)
    deviation = jnp.mean((attended - centre) ** 2, axis=-1, keepdims=True)
    gated = (
        (attended - centre)
        * lax.rsqrt(deviation + 1e-05)
        * out_gain[None]
        * update_gate.astype(jnp.float32)
    )
    gated = gated.astype(jnp.bfloat16)
    columns = lax.all_to_all(w_out, "narrow", split_axis=2, concat_axis=0, tiled=True)
    summed = jnp.einsum(
        "rhc,hcd->rd",
        lax.all_gather(gated, "narrow", axis=1, tiled=True),
        columns,
        preferred_element_type=jnp.float32,
    )
    share = summed.shape[1]
    own_cols = lax.dynamic_slice_in_dim(events_f, lax.axis_index("narrow") * share, share, 1)
    return (own_cols + summed).astype(jnp.bfloat16)


def solution(mesh):
    in_specs = (
        P("wide", None),
        P(),
        P(),
        P(None, "narrow", None),
        P("narrow", None),
        P("narrow", None, None),
    )
    out_specs = P("wide", "narrow")
    return jax.shard_map(
        on_device, mesh=mesh, in_specs=in_specs, out_specs=out_specs, check_vma=False
    )
```

profile of v0, /device:TPU:3, one launch (start us, length us, event | category | flops | bytes accessed | tf_op | source)
XLA Modules:
  0.0 165.2 jit_solution(15008756031488288233)
XLA Ops:
  8.6 2.3 %multiply_reduce_fusion = f32[1024]{0:T(1024)S(1)} fusion(bf16[1024,1024]{1,0:T(8,128)(2,1)} %param.12, f32[1024]{0:T(1024)S(1)} %broadcast_multiply_fusion.1), kind=kLoop, calls=%fused_computation.46 | loop fusion | flops 4193280 | bytes 2105344 | tf_op jit(solution)/shard_map/reduce_sum | solution.py:23
  11.0 3.4 %multiply_convert_fusion = bf16[1024,2,512]{2,0,1:T(8,128)(2,1)S(1)} fusion(bf16[1024,2,512]{2,1,0:T(2,128)(2,1)S(1)} %copy-done, bf16[1024,1024]{1,0:T(8,128)(2,1)S(1)} %copy-done.1, f32[1024]{0:T(1024)S(1)} %copy-done.5, f32[1024]{0:T(1024)S(1)} %add_rsqrt_fusion.1, f32[1024]{0:T(1024)S(1)} %broadcast_multiply_fusion.1), kind=kOutput, calls=%fused_computation.44 | convolution fusion | flops 2157969408 | bytes 6303744 | tf_op jit(solution)/shard_map/rd,dhc->rhc/dot_general | solution.py:25
  17.6 12.9 %while.56 = (s32[]{:T(128)}, f32[1024,2,128]{0,2,1:T(8,128)}, s32[2]{0:T(128)S(1)}, bf16[1024,2,128]{0,2,1:T(8,128)(2,1)S(1)}, s32[24]{0:T(128)S(1)}, /*index=5*...) while((s32[]{:T(128)}, f32[1024,2,128]{0,2,1:T(8,128)}, ...), condition=%wide.region_6.7_spmd.clone.clone.clone, body=%wide.region_4.6_spmd.clone.clone.clone.sunk | while | flops 546871296 | bytes 4219704 | solution.py:66
  19.6 4.2 %fusion.65 = f32[1024,2,128]{0,2,1:T(8,128)} fusion(bf16[1024,2,128]{2,0,1:T(8,128)(2,1)} %get-tuple-element.781, pred[1024,512]{0,1:T(8,128)(4,1)S(1)} %and_and_fusion.4, f32[1024,2,128]{0,2,1:T(8,128)} %get-tuple-element.761, pred[]{:T(512)S(6)} %compare.5, bf16[1024,2,128]{2,0,1:T(8,128)(2,1)} %get-tuple-element.780, s32[]{:T(128)S(6)} %select_n.48, ...), kind=kOutput, calls=%fused_computation.33.clone.1 | convolution fusion | flops 544735232 | bytes 3671552 | tf_op jit(solution)/shard_map/while/body/eval_jaxpr/hrk,khc->rhc/dot_general | solution.py:61
  25.9 4.6 %fusion.65 = f32[1024,2,128]{0,2,1:T(8,128)} fusion(bf16[1024,2,128]{2,0,1:T(8,128)(2,1)} %get-tuple-element.781, pred[1024,512]{0,1:T(8,128)(4,1)S(1)} %and_and_fusion.4, f32[1024,2,128]{0,2,1:T(8,128)} %get-tuple-element.761, pred[]{:T(512)S(6)} %compare.5, bf16[1024,2,128]{2,0,1:T(8,128)(2,1)} %get-tuple-element.780, s32[]{:T(128)S(6)} %select_n.48, ...), kind=kOutput, calls=%fused_computation.33.clone.1 | convolution fusion | flops 544735232 | bytes 3671552 | tf_op jit(solution)/shard_map/while/body/eval_jaxpr/hrk,khc->rhc/dot_general | solution.py:61
  30.5 62.6 %while.55 = (s32[]{:T(128)}, bf16[1024,2,128]{2,0,1:T(8,128)(2,1)}, bf16[1024,2,128]{0,2,1:T(8,128)(2,1)S(1)}, f32[1024,2,128]{0,2,1:T(8,128)}, s32[]{:T(128)}, ...) while((s32[]{:T(128)}, bf16[1024,2,128]{2,0,1:T(8,128)(2,1)}, ...), condition=%wide.region_11.12_spmd.clone.clone, body=%wide.region_7.11_spmd.clone.clone.sunk | while | flops 546609152 | bytes 10511020 | solution.py:82
  30.5 3.7 %collective-permute-start = (bf16[1024,2,128]{2,0,1:T(8,128)(2,1)}, bf16[1024,2,128]{2,0,1:T(8,128)(2,1)S(1)}, u32[]{:S(2)}, u32[]{:S(2)}) collective-permute-start(bf16[1024,2,128]{2,0,1:T(8,128)(2,1)} %get-tuple-element.802), channel_id=1, source_target_pairs={{0,4},{4,8},{8,12},{12,16},{16,20},{20,24},{24,28},{1,5},{5,9},{9,... | collective-permute-start | bytes 1572872 | tf_op jit(solution)/shard_map/while/body/eval_jaxpr/ppermute | solution.py:10
  36.1 4.5 %collective-permute-done = bf16[1024,2,128]{2,0,1:T(8,128)(2,1)S(1)} collective-permute-done((bf16[1024,2,128]{2,0,1:T(8,128)(2,1)}, bf16[1024,2,128]{2,0,1:T(8,128)(2,1)S(1)}, u32[]{:S(2)}, u32[]{:S(2)}) %collective-permute-start) | collective-permute-done | bytes 524320 | tf_op jit(solution)/shard_map/while/body/eval_jaxpr/ppermute | solution.py:10
  40.6 5.5 %collective-permute-done.1 = bf16[1024,2,128]{0,2,1:T(8,128)(2,1)} collective-permute-done((bf16[1024,2,128]{0,2,1:T(8,128)(2,1)S(1)}, bf16[1024,2,128]{0,2,1:T(8,128)(2,1)}, u32[]{:S(2)}, u32[]{:S(2)}) %collective-permute-start.1) | collective-permute-done | bytes 524320 | tf_op jit(solution)/shard_map/while/body/eval_jaxpr/ppermute | solution.py:10
  46.1 13.0 %while.57 = (s32[]{:T(128)}, f32[1024,2,128]{0,2,1:T(8,128)}, s32[2]{0:T(128)S(1)}, bf16[1024,2,128]{0,2,1:T(8,128)(2,1)}, s32[24]{0:T(128)S(1)}, /*index=5*/s32...) while((s32[]{:T(128)}, f32[1024,2,128]{0,2,1:T(8,128)}, ...), condition=%wide.region_10.10_spmd, body=%wide.region_8.9_spmd.sunk | while | flops 546608128 | bytes 4215091 | solution.py:66
  48.0 4.6 %fusion.69 = f32[1024,2,128]{0,2,1:T(8,128)} fusion(f32[1024,2,128]{0,2,1:T(8,128)} %get-tuple-element.720, bf16[1024,2,128]{2,0,1:T(8,128)(2,1)} %get-tuple-element.742, pred[1024,512]{0,1:T(8,128)(4,1)S(1)} %and_and_fusion.5, bf16[1024,2,128]{2,0,1:T(8,128)(2,1)S(1)} %get-tuple-element.741, s32[]{:T(128)S(6)} %select_n.50, ...), kind=kOutput, calls=%fused_computation.12.clone.1 | convolution fusion | flops 544473088 | bytes 3671040 | tf_op jit(solution)/shard_map/while/body/eval_jaxpr/while/body/eval_jaxpr/hrk,khc->rhc/dot_general | solution.py:61
  54.5 4.6 %fusion.69 = f32[1024,2,128]{0,2,1:T(8,128)} fusion(f32[1024,2,128]{0,2,1:T(8,128)} %get-tuple-element.720, bf16[1024,2,128]{2,0,1:T(8,128)(2,1)} %get-tuple-element.742, pred[1024,512]{0,1:T(8,128)(4,1)S(1)} %and_and_fusion.5, bf16[1024,2,128]{2,0,1:T(8,128)(2,1)S(1)} %get-tuple-element.741, s32[]{:T(128)S(6)} %select_n.50, ...), kind=kOutput, calls=%fused_computation.12.clone.1 | convolution fusion | flops 544473088 | bytes 3671040 | tf_op jit(solution)/shard_map/while/body/eval_jaxpr/while/body/eval_jaxpr/hrk,khc->rhc/dot_general | solution.py:61
  60.9 5.4 %collective-permute-start = (bf16[1024,2,128]{2,0,1:T(8,128)(2,1)}, bf16[1024,2,128]{2,0,1:T(8,128)(2,1)S(1)}, u32[]{:S(2)}, u32[]{:S(2)}) collective-permute-start(bf16[1024,2,128]{2,0,1:T(8,128)(2,1)} %get-tuple-element.802), channel_id=1, source_target_pairs={{0,4},{4,8},{8,12},{12,16},{16,20},{20,24},{24,28},{1,5},{5,9},{9,... | collective-permute-start | bytes 1572872 | tf_op jit(solution)/shard_map/while/body/eval_jaxpr/ppermute | solution.py:10
  68.3 4.5 %collective-permute-done = bf16[1024,2,128]{2,0,1:T(8,128)(2,1)S(1)} collective-permute-done((bf16[1024,2,128]{2,0,1:T(8,128)(2,1)}, bf16[1024,2,128]{2,0,1:T(8,128)(2,1)S(1)}, u32[]{:S(2)}, u32[]{:S(2)}) %collective-permute-start) | collective-permute-done | bytes 524320 | tf_op jit(solution)/shard_map/while/body/eval_jaxpr/ppermute | solution.py:10
  72.7 5.5 %collective-permute-done.1 = bf16[1024,2,128]{0,2,1:T(8,128)(2,1)} collective-permute-done((bf16[1024,2,128]{0,2,1:T(8,128)(2,1)S(1)}, bf16[1024,2,128]{0,2,1:T(8,128)(2,1)}, u32[]{:S(2)}, u32[]{:S(2)}) %collective-permute-start.1) | collective-permute-done | bytes 524320 | tf_op jit(solution)/shard_map/while/body/eval_jaxpr/ppermute | solution.py:10
  78.3 13.0 %while.57 = (s32[]{:T(128)}, f32[1024,2,128]{0,2,1:T(8,128)}, s32[2]{0:T(128)S(1)}, bf16[1024,2,128]{0,2,1:T(8,128)(2,1)}, s32[24]{0:T(128)S(1)}, /*index=5*/s32...) while((s32[]{:T(128)}, f32[1024,2,128]{0,2,1:T(8,128)}, ...), condition=%wide.region_10.10_spmd, body=%wide.region_8.9_spmd.sunk | while | flops 546608128 | bytes 4215091 | solution.py:66
  80.2 4.6 %fusion.69 = f32[1024,2,128]{0,2,1:T(8,128)} fusion(f32[1024,2,128]{0,2,1:T(8,128)} %get-tuple-element.720, bf16[1024,2,128]{2,0,1:T(8,128)(2,1)} %get-tuple-element.742, pred[1024,512]{0,1:T(8,128)(4,1)S(1)} %and_and_fusion.5, bf16[1024,2,128]{2,0,1:T(8,128)(2,1)S(1)} %get-tuple-element.741, s32[]{:T(128)S(6)} %select_n.50, ...), kind=kOutput, calls=%fused_computation.12.clone.1 | convolution fusion | flops 544473088 | bytes 3671040 | tf_op jit(solution)/shard_map/while/body/eval_jaxpr/while/body/eval_jaxpr/hrk,khc->rhc/dot_general | solution.py:61
  86.7 4.6 %fusion.69 = f32[1024,2,128]{0,2,1:T(8,128)} fusion(f32[1024,2,128]{0,2,1:T(8,128)} %get-tuple-element.720, bf16[1024,2,128]{2,0,1:T(8,128)(2,1)} %get-tuple-element.742, pred[1024,512]{0,1:T(8,128)(4,1)S(1)} %and_and_fusion.5, bf16[1024,2,128]{2,0,1:T(8,128)(2,1)S(1)} %get-tuple-element.741, s32[]{:T(128)S(6)} %select_n.50, ...), kind=kOutput, calls=%fused_computation.12.clone.1 | convolution fusion | flops 544473088 | bytes 3671040 | tf_op jit(solution)/shard_map/while/body/eval_jaxpr/while/body/eval_jaxpr/hrk,khc->rhc/dot_general | solution.py:61
  96.7 2.4 %multiply_convert_fusion.2 = bf16[1024,2,128]{2,0,1:T(8,128)(2,1)} fusion(f32[1024,2,128]{2,0,1:T(8,128)S(1)} %copy.38, bf16[1024,2,512]{2,0,1:T(8,128)(2,1)} %copy-done.2, f32[2,128]{1,0:T(2,128)S(1)} %copy-done.3, f32[1024,2]{0,1:T(2,128)S(1)} %add_rsqrt_fusion, f32[1024,2]{0,1:T(2,128)S(1)} %broadcast_multiply_fusion), kind=kLoop, calls=%fused_computation.57 | loop fusion | flops 1572864 | bytes 2114560 | tf_op jit(solution)/shard_map/convert_element_type | solution.py:91
  101.1 4.6 %all-to-all-start = ((bf16[2,128,1024]{1,0,2:T(2,128)(2,1)}), bf16[2,128,1024]{1,0,2:T(2,128)(2,1)S(1)}, u32[]{:S(2)}, u32[]{:S(2)}) async-start(bf16[2,128,1024]{1,0,2:T(2,128)(2,1)} %copy.39), calls=%async_computation | async-start | bytes 1048576 | tf_op jit(solution)/shard_map/all_to_all | solution.py:92
  105.7 4.0 %convert_element_type.33 = f32[1024,1024]{1,0:T(8,128)} convert(bf16[1024,1024]{1,0:T(8,128)(2,1)} %param.12) | non-fusion elementwise | flops 1048576 | bytes 6291456 | tf_op jit(solution)/shard_map/convert_element_type | solution.py:21
  109.6 17.5 %all-to-all-done = bf16[2,128,1024]{1,0,2:T(2,128)(2,1)S(1)} async-done(((bf16[2,128,1024]{1,0,2:T(2,128)(2,1)}), bf16[2,128,1024]{1,0,2:T(2,128)(2,1)S(1)}, u32[]{:S(2)}, u32[]{:S(2)}) %all-to-all-start) | async-done | bytes 524320 | tf_op jit(solution)/shard_map/all_to_all | solution.py:92
  127.5 27.4 %all-gather.2.cloned.1.call-done = bf16[1024,8,128]{2,0,1:T(8,128)(2,1)} async-done(((bf16[1024,2,128]{2,0,1:T(8,128)(2,1)}), bf16[1024,8,128]{2,0,1:T(8,128)(2,1)}) %all-gather.2.cloned.1.call-update) | async-done | bytes 2097168 | tf_op jit(solution)/shard_map/all_gather | solution.py:95
  154.9 3.4 %fusion.48 = bf16[1024,256]{1,0:T(8,128)(2,1)} fusion(bf16[1024,8,128]{2,0,1:T(8,128)(2,1)} %all-gather.2.cloned.1.call-done, bf16[8,128,256]{2,1,0:T(8,128)(2,1)S(1)} %bitcast.89, f32[1024,1024]{1,0:T(8,128)} %convert_element_type.33, s32[]{:T(128)S(6)} %select_n.18), kind=kOutput, calls=%fused_computation.56 | convolution fusion | flops 537395200 | bytes 4194308 | tf_op jit(solution)/shard_map/rhc,hcd->rd/dot_general | solution.py:93
  (75 shorter events, 26.3 us)
Async XLA Ops:
  6.5 4.4 %copy-start = (bf16[1024,2,512]{2,1,0:T(2,128)(2,1)S(1)}, bf16[1024,2,512]{2,1,0:T(2,128)(2,1)}, u32[]{:S(2)}) copy-start(bf16[1024,2,512]{2,1,0:T(2,128)(2,1)} %param.15) | copy-start | bytes 6291460
  6.5 4.4 %copy-start.5 = (f32[1024]{0:T(1024)S(1)}, f32[1024]{0:T(1024)}, u32[]{:S(2)}) copy-start(f32[1024]{0:T(1024)} %param.14) | copy-start | bytes 12292
  6.5 148.4 %all-gather.2.cloned.1.call-start = ((), (), s32[]{:S(2)}) async-start(), calls=%async_computation.1 | async-start | bytes 2621440 | tf_op jit(solution)/shard_map/all_gather | solution.py:95
  6.5 4.4 %copy-start.1 = (bf16[1024,1024]{1,0:T(8,128)(2,1)S(1)}, bf16[1024,1024]{1,0:T(8,128)(2,1)}, u32[]{:S(2)}) copy-start(bf16[1024,1024]{1,0:T(8,128)(2,1)} %param.12) | copy-start | bytes 6291460
  14.4 1.4 copy-start.2
  15.7 1.5 copy-start.4
  30.5 10.1 %collective-permute-start = (bf16[1024,2,128]{2,0,1:T(8,128)(2,1)}, bf16[1024,2,128]{2,0,1:T(8,128)(2,1)S(1)}, u32[]{:S(2)}, u32[]{:S(2)}) collective-permute-start(bf16[1024,2,128]{2,0,1:T(8,128)(2,1)} %get-tuple-element.802), channel_id=1, source_target_pairs={{0,4},{4,8},{8,12},{12,16},{16,20},{20,24},{24,28},{1,5},{5,9},{9,... | collective-permute-start | bytes 1572872 | tf_op jit(solution)/shard_map/while/body/eval_jaxpr/ppermute | solution.py:10
  34.2 11.9 %collective-permute-start.1 = (bf16[1024,2,128]{0,2,1:T(8,128)(2,1)S(1)}, bf16[1024,2,128]{0,2,1:T(8,128)(2,1)}, u32[]{:S(2)}, u32[]{:S(2)}) collective-permute-start(bf16[1024,2,128]{0,2,1:T(8,128)(2,1)S(1)} %get-tuple-element.803), channel_id=1, source_target_pairs={{0,4},{4,8},{8,12},{12,16},{16,20},{20,24},{24,28},{1,5},{5,9},{9,... | collective-permute-start | bytes 1572872 | tf_op jit(solution)/shard_map/while/body/eval_jaxpr/ppermute | solution.py:10
  60.9 11.8 %collective-permute-start = (bf16[1024,2,128]{2,0,1:T(8,128)(2,1)}, bf16[1024,2,128]{2,0,1:T(8,128)(2,1)S(1)}, u32[]{:S(2)}, u32[]{:S(2)}) collective-permute-start(bf16[1024,2,128]{2,0,1:T(8,128)(2,1)} %get-tuple-element.802), channel_id=1, source_target_pairs={{0,4},{4,8},{8,12},{12,16},{16,20},{20,24},{24,28},{1,5},{5,9},{9,... | collective-permute-start | bytes 1572872 | tf_op jit(solution)/shard_map/while/body/eval_jaxpr/ppermute | solution.py:10
  66.3 11.9 %collective-permute-start.1 = (bf16[1024,2,128]{0,2,1:T(8,128)(2,1)S(1)}, bf16[1024,2,128]{0,2,1:T(8,128)(2,1)}, u32[]{:S(2)}, u32[]{:S(2)}) collective-permute-start(bf16[1024,2,128]{0,2,1:T(8,128)(2,1)S(1)} %get-tuple-element.803), channel_id=1, source_target_pairs={{0,4},{4,8},{8,12},{12,16},{16,20},{20,24},{24,28},{1,5},{5,9},{9,... | collective-permute-start | bytes 1572872 | tf_op jit(solution)/shard_map/while/body/eval_jaxpr/ppermute | solution.py:10
  93.1 3.6 %copy-start.3 = (f32[2,128]{1,0:T(2,128)S(1)}, f32[2,128]{1,0:T(2,128)}, u32[]{:S(2)}) copy-start(f32[2,128]{1,0:T(2,128)} %param.16) | copy-start | bytes 3076
  101.1 26.1 %all-to-all-start = ((bf16[2,128,1024]{1,0,2:T(2,128)(2,1)}), bf16[2,128,1024]{1,0,2:T(2,128)(2,1)S(1)}, u32[]{:S(2)}, u32[]{:S(2)}) async-start(bf16[2,128,1024]{1,0,2:T(2,128)(2,1)} %copy.39), calls=%async_computation | async-start | bytes 1048576 | tf_op jit(solution)/shard_map/all_to_all | solution.py:92
Sparse Core Ops, SparseCore 0:
  99.2 55.7 all-gather.1
where the time goes:
time: 166 us; the launch traced here: 165 us
  waiting for transfers between devices  64.9 us (39%)
  matrix products  33.8 us (20%)
  starting transfers between devices  17.5 us (11%)
  other arithmetic  16.9 us (10%)
  local copies, waits for them, and re-layouts  14.2 us (9%)
  between operations  13.5 us (8%)
  loops' own time  4.27 us (3%)
    all_gather x1, waiting for transfers between devices, on_device(): lax.all_gather(gated, 'narrow', axis=1, tiled=True)  27.4 us
    dot_general x6, matrix products, block_step(): jnp.einsum('hrk,khc->rhc', weights, value_block, preferred_element_type=j...  27.1 us
    ppermute x4, waiting for transfers between devices, from_behind(): lax.ppermute(value, axis, [(source, source + steps) for source in range(i...  20 us
    all_to_all x1, waiting for transfers between devices, on_device(): lax.all_to_all(w_out, 'narrow', split_axis=2, concat_axis=0, tiled=True)  17.5 us
    ppermute x4, starting transfers between devices, from_behind(): lax.ppermute(value, axis, [(source, source + steps) for source in range(i...  12.9 us
    all_to_all x1, starting transfers between devices, on_device(): lax.all_to_all(w_out, 'narrow', split_axis=2, concat_axis=0, tiled=True)  4.59 us
    another operation x3, loops' own time, attend(): lax.scan(block_step, running, jnp.arange(key_count // block_rows, dtype=j...  4.21 us
    convert_element_type x1, other arithmetic, on_device(): events_f = events.astype(jnp.float32)  3.98 us
  transfers between devices with their start and end apart: 6, of which 6 were waited for; matrix products, arithmetic and copies ran while one was open for 4% of the time, Pallas kernels for 0%

commit v1 on v0

--- a/solution.py
+++ b/solution.py
@@ -2,6 +2,30 @@
 import jax.numpy as jnp
 from jax import lax
 from jax.sharding import PartitionSpec as P
+
+
+def panel_supply(own_rows, row_dim):
+    p_next = list(own_rows.shape[1:])
+    p_next[row_dim] *= own_rows.shape[0]
+    later = jnp.moveaxis(own_rows, 0, row_dim).reshape(p_next)
+    return later
+
+
+def link_copies_for(u, dev_axis, out_dim):
+    extent = lax.axis_size(dev_axis)
+    tray = [(ii, (ii + 1) % extent) for ii in range(extent)]
+    block_next, prior = ([], [])
+    shelf = [(k0, it) for it, k0 in tray]
+    for i0 in range(extent - 1):
+        if i0 % 2 == 0:
+            block_next.append(lax.ppermute(block_next[-1] if block_next else u, dev_axis, tray))
+        else:
+            prior.append(lax.ppermute(prior[-1] if prior else u, dev_axis, perm=shelf))
+    now = jnp.stack([*block_next[::-1], u, *prior])
+    vec_out = lax.axis_index(dev_axis) - len(block_next)
+    now = now[(jnp.arange(extent) - vec_out) % extent]
+    all_values = panel_supply(now, out_dim)
+    return all_values
 
 
 def from_behind(value, axis, steps):
@@ -92,7 +116,7 @@
     columns = lax.all_to_all(w_out, "narrow", split_axis=2, concat_axis=0, tiled=True)
     summed = jnp.einsum(
         "rhc,hcd->rd",
-        lax.all_gather(gated, "narrow", axis=1, tiled=True),
+        link_copies_for(gated, "narrow", out_dim=1),
         columns,
         preferred_element_type=jnp.float32,
     )

time: 166 us -> 151 us (0.910)
  the two profiles are of different devices: /device:TPU:3 before, /device:TPU:11 now
where the time goes in v1:
time: 151 us; the launch traced here: 150 us
  waiting for transfers between devices  55.9 us (37%)
  matrix products  33.7 us (22%)
  starting transfers between devices  19.3 us (13%)
  other arithmetic  18.5 us (12%)
  local copies, waits for them, and re-layouts  18.2 us (12%)
  loops' own time  4.28 us (3%)
    dot_general x6, matrix products, block_step(): jnp.einsum('hrk,khc->rhc', weights, value_block, preferred_element_type=j...  27 us
    ppermute x4, waiting for transfers between devices, from_behind(): lax.ppermute(value, axis, [(source, source + steps) for source in range(i...  20 us
    all_to_all x1, waiting for transfers between devices, on_device(): lax.all_to_all(w_out, 'narrow', split_axis=2, concat_axis=0, tiled=True)  16.3 us
    ppermute x1, waiting for transfers between devices, link_copies_for(): prior.append(lax.ppermute(prior[-1] if prior else u, dev_axis, perm=shelf))  13.5 us
    ppermute x4, starting transfers between devices, from_behind(): lax.ppermute(value, axis, [(source, source + steps) for source in range(i...  12.9 us
    ppermute x2, waiting for transfers between devices, link_copies_for(): lax.ppermute(block_next[-1] if block_next else u, dev_axis, tray)  6.14 us
    another operation x3, loops' own time, attend(): lax.scan(block_step, running, jnp.arange(key_count // block_rows, dtype=j...  4.21 us
    convert_element_type x1, other arithmetic, on_device(): events_f = events.astype(jnp.float32)  3.98 us
  transfers between devices with their start and end apart: 8, of which 7 were waited for; matrix products, arithmetic and copies ran while one was open for 4% of the time, Pallas kernels for 0%

profile of v1, /device:TPU:11, one launch (start us, length us, event | category | flops | bytes accessed | tf_op | source)
XLA Modules:
  0.0 150.0 jit_solution(9890938253040858357)
XLA Ops:
  3.1 3.4 %multiply_convert_fusion = bf16[1024,2,512]{2,0,1:T(8,128)(2,1)S(1)} fusion(bf16[1024,2,512]{2,1,0:T(2,128)(2,1)S(1)} %copy-done, bf16[1024,1024]{1,0:T(8,128)(2,1)S(1)} %copy-done.1, f32[1024]{0:T(1024)S(1)} %copy-done.5, f32[1024]{0:T(1024)S(1)} %add_rsqrt_fusion.1, f32[1024]{0:T(1024)S(1)} %broadcast_multiply_fusion.1), kind=kOutput, calls=%fused_computation.45 | convolution fusion | flops 2157969408 | bytes 6303744 | tf_op jit(solution)/shard_map/rd,dhc->rhc/dot_general | solution.py:49
  9.7 12.9 %while.56 = (s32[]{:T(128)}, f32[1024,2,128]{0,2,1:T(8,128)}, s32[2]{0:T(128)S(1)}, bf16[1024,2,128]{0,2,1:T(8,128)(2,1)S(1)}, s32[24]{0:T(128)S(1)}, /*index=5*...) while((s32[]{:T(128)}, f32[1024,2,128]{0,2,1:T(8,128)}, ...), condition=%wide.region_6.7_spmd.clone.clone.clone, body=%wide.region_4.6_spmd.clone.clone.clone.sunk | while | flops 546871296 | bytes 4219704 | solution.py:90
  11.8 4.2 %fusion.67 = f32[1024,2,128]{0,2,1:T(8,128)} fusion(bf16[1024,2,128]{2,0,1:T(8,128)(2,1)} %get-tuple-element.781, pred[1024,512]{0,1:T(8,128)(4,1)S(1)} %and_and_fusion.4, f32[1024,2,128]{0,2,1:T(8,128)} %get-tuple-element.761, pred[]{:T(512)S(6)} %compare.12, bf16[1024,2,128]{2,0,1:T(8,128)(2,1)} %get-tuple-element.780, s32[]{:T(128)S(6)} %select_n.82, ...), kind=kOutput, calls=%fused_computation.34.clone.1 | convolution fusion | flops 544735232 | bytes 3671552 | tf_op jit(solution)/shard_map/while/body/eval_jaxpr/hrk,khc->rhc/dot_general | solution.py:85
  18.0 4.6 %fusion.67 = f32[1024,2,128]{0,2,1:T(8,128)} fusion(bf16[1024,2,128]{2,0,1:T(8,128)(2,1)} %get-tuple-element.781, pred[1024,512]{0,1:T(8,128)(4,1)S(1)} %and_and_fusion.4, f32[1024,2,128]{0,2,1:T(8,128)} %get-tuple-element.761, pred[]{:T(512)S(6)} %compare.12, bf16[1024,2,128]{2,0,1:T(8,128)(2,1)} %get-tuple-element.780, s32[]{:T(128)S(6)} %select_n.82, ...), kind=kOutput, calls=%fused_computation.34.clone.1 | convolution fusion | flops 544735232 | bytes 3671552 | tf_op jit(solution)/shard_map/while/body/eval_jaxpr/hrk,khc->rhc/dot_general | solution.py:85
  22.6 62.5 %while.55 = (s32[]{:T(128)}, bf16[1024,2,128]{2,0,1:T(8,128)(2,1)}, bf16[1024,2,128]{0,2,1:T(8,128)(2,1)S(1)}, f32[1024,2,128]{0,2,1:T(8,128)}, s32[]{:T(128)}, ...) while((s32[]{:T(128)}, bf16[1024,2,128]{2,0,1:T(8,128)(2,1)}, ...), condition=%wide.region_11.12_spmd.clone.clone, body=%wide.region_7.11_spmd.clone.clone.sunk | while | flops 546609152 | bytes 10511020 | solution.py:106
  22.6 3.7 %collective-permute-start = (bf16[1024,2,128]{2,0,1:T(8,128)(2,1)}, bf16[1024,2,128]{2,0,1:T(8,128)(2,1)S(1)}, u32[]{:S(2)}, u32[]{:S(2)}) collective-permute-start(bf16[1024,2,128]{2,0,1:T(8,128)(2,1)} %get-tuple-element.802), channel_id=1, source_target_pairs={{0,4},{4,8},{8,12},{12,16},{16,20},{20,24},{24,28},{1,5},{5,9},{9,... | collective-permute-start | bytes 1572872 | tf_op jit(solution)/shard_map/while/body/eval_jaxpr/ppermute | solution.py:34
  28.2 4.5 %collective-permute-done = bf16[1024,2,128]{2,0,1:T(8,128)(2,1)S(1)} collective-permute-done((bf16[1024,2,128]{2,0,1:T(8,128)(2,1)}, bf16[1024,2,128]{2,0,1:T(8,128)(2,1)S(1)}, u32[]{:S(2)}, u32[]{:S(2)}) %collective-permute-start) | collective-permute-done | bytes 524320 | tf_op jit(solution)/shard_map/while/body/eval_jaxpr/ppermute | solution.py:34
  32.7 5.5 %collective-permute-done.1 = bf16[1024,2,128]{0,2,1:T(8,128)(2,1)} collective-permute-done((bf16[1024,2,128]{0,2,1:T(8,128)(2,1)S(1)}, bf16[1024,2,128]{0,2,1:T(8,128)(2,1)}, u32[]{:S(2)}, u32[]{:S(2)}) %collective-permute-start.1) | collective-permute-done | bytes 524320 | tf_op jit(solution)/shard_map/while/body/eval_jaxpr/ppermute | solution.py:34
  38.2 13.0 %while.57 = (s32[]{:T(128)}, f32[1024,2,128]{0,2,1:T(8,128)}, s32[2]{0:T(128)S(1)}, bf16[1024,2,128]{0,2,1:T(8,128)(2,1)}, s32[24]{0:T(128)S(1)}, /*index=5*/s32...) while((s32[]{:T(128)}, f32[1024,2,128]{0,2,1:T(8,128)}, ...), condition=%wide.region_10.10_spmd, body=%wide.region_8.9_spmd.sunk | while | flops 546608128 | bytes 4215091 | solution.py:90
  40.1 4.6 %fusion.71 = f32[1024,2,128]{0,2,1:T(8,128)} fusion(f32[1024,2,128]{0,2,1:T(8,128)} %get-tuple-element.720, bf16[1024,2,128]{2,0,1:T(8,128)(2,1)} %get-tuple-element.742, pred[1024,512]{0,1:T(8,128)(4,1)S(1)} %and_and_fusion.5, bf16[1024,2,128]{2,0,1:T(8,128)(2,1)S(1)} %get-tuple-element.741, s32[]{:T(128)S(6)} %select_n.84, ...), kind=kOutput, calls=%fused_computation.13.clone.1 | convolution fusion | flops 544473088 | bytes 3671040 | tf_op jit(solution)/shard_map/while/body/eval_jaxpr/while/body/eval_jaxpr/hrk,khc->rhc/dot_general | solution.py:85
  46.6 4.6 %fusion.71 = f32[1024,2,128]{0,2,1:T(8,128)} fusion(f32[1024,2,128]{0,2,1:T(8,128)} %get-tuple-element.720, bf16[1024,2,128]{2,0,1:T(8,128)(2,1)} %get-tuple-element.742, pred[1024,512]{0,1:T(8,128)(4,1)S(1)} %and_and_fusion.5, bf16[1024,2,128]{2,0,1:T(8,128)(2,1)S(1)} %get-tuple-element.741, s32[]{:T(128)S(6)} %select_n.84, ...), kind=kOutput, calls=%fused_computation.13.clone.1 | convolution fusion | flops 544473088 | bytes 3671040 | tf_op jit(solution)/shard_map/while/body/eval_jaxpr/while/body/eval_jaxpr/hrk,khc->rhc/dot_general | solution.py:85
  53.0 5.4 %collective-permute-start = (bf16[1024,2,128]{2,0,1:T(8,128)(2,1)}, bf16[1024,2,128]{2,0,1:T(8,128)(2,1)S(1)}, u32[]{:S(2)}, u32[]{:S(2)}) collective-permute-start(bf16[1024,2,128]{2,0,1:T(8,128)(2,1)} %get-tuple-element.802), channel_id=1, source_target_pairs={{0,4},{4,8},{8,12},{12,16},{16,20},{20,24},{24,28},{1,5},{5,9},{9,... | collective-permute-start | bytes 1572872 | tf_op jit(solution)/shard_map/while/body/eval_jaxpr/ppermute | solution.py:34
  60.3 4.5 %collective-permute-done = bf16[1024,2,128]{2,0,1:T(8,128)(2,1)S(1)} collective-permute-done((bf16[1024,2,128]{2,0,1:T(8,128)(2,1)}, bf16[1024,2,128]{2,0,1:T(8,128)(2,1)S(1)}, u32[]{:S(2)}, u32[]{:S(2)}) %collective-permute-start) | collective-permute-done | bytes 524320 | tf_op jit(solution)/shard_map/while/body/eval_jaxpr/ppermute | solution.py:34
  64.8 5.5 %collective-permute-done.1 = bf16[1024,2,128]{0,2,1:T(8,128)(2,1)} collective-permute-done((bf16[1024,2,128]{0,2,1:T(8,128)(2,1)S(1)}, bf16[1024,2,128]{0,2,1:T(8,128)(2,1)}, u32[]{:S(2)}, u32[]{:S(2)}) %collective-permute-start.1) | collective-permute-done | bytes 524320 | tf_op jit(solution)/shard_map/while/body/eval_jaxpr/ppermute | solution.py:34
  70.3 13.0 %while.57 = (s32[]{:T(128)}, f32[1024,2,128]{0,2,1:T(8,128)}, s32[2]{0:T(128)S(1)}, bf16[1024,2,128]{0,2,1:T(8,128)(2,1)}, s32[24]{0:T(128)S(1)}, /*index=5*/s32...) while((s32[]{:T(128)}, f32[1024,2,128]{0,2,1:T(8,128)}, ...), condition=%wide.region_10.10_spmd, body=%wide.region_8.9_spmd.sunk | while | flops 546608128 | bytes 4215091 | solution.py:90
  72.2 4.6 %fusion.71 = f32[1024,2,128]{0,2,1:T(8,128)} fusion(f32[1024,2,128]{0,2,1:T(8,128)} %get-tuple-element.720, bf16[1024,2,128]{2,0,1:T(8,128)(2,1)} %get-tuple-element.742, pred[1024,512]{0,1:T(8,128)(4,1)S(1)} %and_and_fusion.5, bf16[1024,2,128]{2,0,1:T(8,128)(2,1)S(1)} %get-tuple-element.741, s32[]{:T(128)S(6)} %select_n.84, ...), kind=kOutput, calls=%fused_computation.13.clone.1 | convolution fusion | flops 544473088 | bytes 3671040 | tf_op jit(solution)/shard_map/while/body/eval_jaxpr/while/body/eval_jaxpr/hrk,khc->rhc/dot_general | solution.py:85
  78.7 4.6 %fusion.71 = f32[1024,2,128]{0,2,1:T(8,128)} fusion(f32[1024,2,128]{0,2,1:T(8,128)} %get-tuple-element.720, bf16[1024,2,128]{2,0,1:T(8,128)(2,1)} %get-tuple-element.742, pred[1024,512]{0,1:T(8,128)(4,1)S(1)} %and_and_fusion.5, bf16[1024,2,128]{2,0,1:T(8,128)(2,1)S(1)} %get-tuple-element.741, s32[]{:T(128)S(6)} %select_n.84, ...), kind=kOutput, calls=%fused_computation.13.clone.1 | convolution fusion | flops 544473088 | bytes 3671040 | tf_op jit(solution)/shard_map/while/body/eval_jaxpr/while/body/eval_jaxpr/hrk,khc->rhc/dot_general | solution.py:85
  94.4 3.7 %all-to-all-start = ((bf16[2,128,1024]{1,0,2:T(2,128)(2,1)}), bf16[2,128,1024]{1,0,2:T(2,128)(2,1)S(1)}, u32[]{:S(2)}, u32[]{:S(2)}) async-start(bf16[2,128,1024]{1,0,2:T(2,128)(2,1)} %copy.39), calls=%async_computation | async-start | bytes 1048576 | tf_op jit(solution)/shard_map/all_to_all | solution.py:116
  98.1 6.1 %collective-permute-done.2 = bf16[1024,2,128]{2,0,1:T(8,128)(2,1)} collective-permute-done((bf16[1024,2,128]{2,0,1:T(8,128)(2,1)}, bf16[1024,2,128]{2,0,1:T(8,128)(2,1)}, u32[]{:S(2)}, u32[]{:S(2)}) %collective-permute-start.2) | collective-permute-done | bytes 524320 | tf_op jit(solution)/shard_map/ppermute | solution.py:21
  105.6 4.0 %convert_element_type.33 = f32[1024,1024]{1,0:T(8,128)} convert(bf16[1024,1024]{1,0:T(8,128)(2,1)} %param.12) | non-fusion elementwise | flops 1048576 | bytes 6291456 | tf_op jit(solution)/shard_map/convert_element_type | solution.py:45
  109.6 16.3 %all-to-all-done = bf16[2,128,1024]{1,0,2:T(2,128)(2,1)S(1)} async-done(((bf16[2,128,1024]{1,0,2:T(2,128)(2,1)}), bf16[2,128,1024]{1,0,2:T(2,128)(2,1)S(1)}, u32[]{:S(2)}, u32[]{:S(2)}) %all-to-all-start) | async-done | bytes 524320 | tf_op jit(solution)/shard_map/all_to_all | solution.py:116
  126.3 13.5 %collective-permute-done.4 = bf16[1024,2,128]{2,0,1:T(8,128)(2,1)} collective-permute-done((bf16[1024,2,128]{2,0,1:T(8,128)(2,1)}, bf16[1024,2,128]{2,0,1:T(8,128)(2,1)}, u32[]{:S(2)}, u32[]{:S(2)}) %collective-permute-start.4) | collective-permute-done | bytes 524320 | tf_op jit(solution)/shard_map/ppermute | solution.py:23
  142.9 3.7 %gather_fusion = bf16[4,1024,2,128]{3,1,2,0:T(8,128)(2,1)} fusion(bf16[4,1024,2,128]{3,1,2,0:T(8,128)(2,1)} %pad_maximum_fusion, s32[1024]{0:T(1024)S(1)} %pad_clamp_fusion), kind=kCustom, calls=%fused_computation | custom fusion | bytes 4194320 | tf_op jit(solution)/shard_map/gather | solution.py:26
  146.6 3.4 %fusion.48 = bf16[1024,256]{1,0:T(8,128)(2,1)} fusion(bf16[1024,8,128]{2,0,1:T(8,128)(2,1)} %bitcast.97, bf16[8,128,256]{2,1,0:T(8,128)(2,1)S(1)} %bitcast.99, f32[1024,1024]{1,0:T(8,128)} %convert_element_type.33, s32[]{:T(128)S(6)} %select_n.42), kind=kOutput, calls=%fused_computation.58 | convolution fusion | flops 537395200 | bytes 4194308 | tf_op jit(solution)/shard_map/rhc,hcd->rd/dot_general | solution.py:117
  (82 shorter events, 35.4 us)
Async XLA Ops:
  0.0 3.1 %copy-start = (bf16[1024,2,512]{2,1,0:T(2,128)(2,1)S(1)}, bf16[1024,2,512]{2,1,0:T(2,128)(2,1)}, u32[]{:S(2)}) copy-start(bf16[1024,2,512]{2,1,0:T(2,128)(2,1)} %param.15) | copy-start | bytes 6291460
  0.0 2.4 %copy-start.1 = (bf16[1024,1024]{1,0:T(8,128)(2,1)S(1)}, bf16[1024,1024]{1,0:T(8,128)(2,1)}, u32[]{:S(2)}) copy-start(bf16[1024,1024]{1,0:T(8,128)(2,1)} %param.12) | copy-start | bytes 6291460
  0.0 3.1 %copy-start.5 = (f32[1024]{0:T(1024)S(1)}, f32[1024]{0:T(1024)}, u32[]{:S(2)}) copy-start(f32[1024]{0:T(1024)} %param.14) | copy-start | bytes 12292
  6.5 1.4 copy-start.2
  7.8 1.5 copy-start.4
  22.6 10.1 %collective-permute-start = (bf16[1024,2,128]{2,0,1:T(8,128)(2,1)}, bf16[1024,2,128]{2,0,1:T(8,128)(2,1)S(1)}, u32[]{:S(2)}, u32[]{:S(2)}) collective-permute-start(bf16[1024,2,128]{2,0,1:T(8,128)(2,1)} %get-tuple-element.802), channel_id=1, source_target_pairs={{0,4},{4,8},{8,12},{12,16},{16,20},{20,24},{24,28},{1,5},{5,9},{9,... | collective-permute-start | bytes 1572872 | tf_op jit(solution)/shard_map/while/body/eval_jaxpr/ppermute | solution.py:34
  26.3 11.9 %collective-permute-start.1 = (bf16[1024,2,128]{0,2,1:T(8,128)(2,1)S(1)}, bf16[1024,2,128]{0,2,1:T(8,128)(2,1)}, u32[]{:S(2)}, u32[]{:S(2)}) collective-permute-start(bf16[1024,2,128]{0,2,1:T(8,128)(2,1)S(1)} %get-tuple-element.803), channel_id=1, source_target_pairs={{0,4},{4,8},{8,12},{12,16},{16,20},{20,24},{24,28},{1,5},{5,9},{9,... | collective-permute-start | bytes 1572872 | tf_op jit(solution)/shard_map/while/body/eval_jaxpr/ppermute | solution.py:34
  53.0 11.8 %collective-permute-start = (bf16[1024,2,128]{2,0,1:T(8,128)(2,1)}, bf16[1024,2,128]{2,0,1:T(8,128)(2,1)S(1)}, u32[]{:S(2)}, u32[]{:S(2)}) collective-permute-start(bf16[1024,2,128]{2,0,1:T(8,128)(2,1)} %get-tuple-element.802), channel_id=1, source_target_pairs={{0,4},{4,8},{8,12},{12,16},{16,20},{20,24},{24,28},{1,5},{5,9},{9,... | collective-permute-start | bytes 1572872 | tf_op jit(solution)/shard_map/while/body/eval_jaxpr/ppermute | solution.py:34
  58.4 11.9 %collective-permute-start.1 = (bf16[1024,2,128]{0,2,1:T(8,128)(2,1)S(1)}, bf16[1024,2,128]{0,2,1:T(8,128)(2,1)}, u32[]{:S(2)}, u32[]{:S(2)}) collective-permute-start(bf16[1024,2,128]{0,2,1:T(8,128)(2,1)S(1)} %get-tuple-element.803), channel_id=1, source_target_pairs={{0,4},{4,8},{8,12},{12,16},{16,20},{20,24},{24,28},{1,5},{5,9},{9,... | collective-permute-start | bytes 1572872 | tf_op jit(solution)/shard_map/while/body/eval_jaxpr/ppermute | solution.py:34
  85.1 3.6 %copy-start.3 = (f32[2,128]{1,0:T(2,128)S(1)}, f32[2,128]{1,0:T(2,128)}, u32[]{:S(2)}) copy-start(f32[2,128]{1,0:T(2,128)} %param.16) | copy-start | bytes 3076
  91.0 13.2 %collective-permute-start.2 = (bf16[1024,2,128]{2,0,1:T(8,128)(2,1)}, bf16[1024,2,128]{2,0,1:T(8,128)(2,1)}, u32[]{:S(2)}, u32[]{:S(2)}) collective-permute-start(bf16[1024,2,128]{2,0,1:T(8,128)(2,1)} %multiply_convert_fusion.2), channel_id=1, source_target_pairs={{0,1},{1,2},{2,3},{3,0},{4,5},{5,6},{6,7},{7,4},{8,9},{9,10},{10,1... | collective-permute-start | bytes 1572872 | tf_op jit(solution)/shard_map/ppermute | solution.py:21
  94.4 31.5 %all-to-all-start = ((bf16[2,128,1024]{1,0,2:T(2,128)(2,1)}), bf16[2,128,1024]{1,0,2:T(2,128)(2,1)S(1)}, u32[]{:S(2)}, u32[]{:S(2)}) async-start(bf16[2,128,1024]{1,0,2:T(2,128)(2,1)} %copy.39), calls=%async_computation | async-start | bytes 1048576 | tf_op jit(solution)/shard_map/all_to_all | solution.py:116
  98.1 41.7 %collective-permute-start.4 = (bf16[1024,2,128]{2,0,1:T(8,128)(2,1)}, bf16[1024,2,128]{2,0,1:T(8,128)(2,1)}, u32[]{:S(2)}, u32[]{:S(2)}) collective-permute-start(bf16[1024,2,128]{2,0,1:T(8,128)(2,1)} %multiply_convert_fusion.2), channel_id=1, source_target_pairs={{1,0},{2,1},{3,2},{0,3},{5,4},{6,5},{7,6},{4,7},{9,8},{10,9},{11,1... | collective-permute-start | bytes 1572872 | tf_op jit(solution)/shard_map/ppermute | solution.py:23
  104.2 35.6 %collective-permute-start.3 = (bf16[1024,2,128]{2,0,1:T(8,128)(2,1)}, bf16[1024,2,128]{2,0,1:T(8,128)(2,1)}, u32[]{:S(2)}, u32[]{:S(2)}) collective-permute-start(bf16[1024,2,128]{2,0,1:T(8,128)(2,1)} %collective-permute-done.2), channel_id=1, source_target_pairs={{0,1},{1,2},{2,3},{3,0},{4,5},{5,6},{6,7},{7,4},{8,9},{9,10},{10,1... | collective-permute-start | bytes 1572872 | tf_op jit(solution)/shard_map/ppermute | solution.py:21
